TPU v7x, 32 devices: a whole 2x2x4 slice. The times are simulated.
32 devices in a mesh: row: 8 (over y, x, core), col: 4 (over z).
Axes of the slice: x: 2, y: 2, z: 4, core: 2. Of those that a mesh axis runs over, the one named last changes fastest.
Arguments:
- inverse_rows: float32 [16384, 16384], P('col', 'row'), may hold values from -0.5 to 0.5
- panels: float32 [4, 16384, 256], P('col', 'row'), may hold values from -0.75 to 0.75
- diag_inverse: float32 [2, 256, 256], replicated, may hold values from -12 to 12
- pattern: int32 [2, 64], replicated, may hold values 0 or 1
- owner_slot: int32 [2], replicated, may hold values from 0 to 3, as said below
Outputs:
- inverse_column: float32 [2, 16384, 256], P(None, 'row')
- inverse_row: float32 [2, 256, 16384], P(None, None, 'col')
- diag_block: float32 [2, 256, 256], replicated
Inputs may be any that keep to these rules, and one draw needn't show every extreme that they name: `owner_slot`: the two supernodes' panels lie in two different slots, one of them the last slot.
All inputs are finite; a program needn't handle non-finite values.
Results may differ from a plain program's by a relative error of at most 0.0001.
Values sent between devices are 32-bit elements; how exact they have to be, the bound alone decides.
A program may use at most 128 MiB of HBM per device.

v0:
```python
import jax
import jax.numpy as jnp
from jax import lax
from jax.sharding import PartitionSpec as P


def from_root(array, axis, root):
    mine = lax.axis_index(axis) == root
    return lax.psum(jnp.where(mine, array, jnp.zeros_like(array)), axis)


def block_mask(pattern_row, start_block, count_blocks, width):
    live = lax.dynamic_slice_in_dim(pattern_row, start_block, count_blocks, 0).astype(jnp.float32)
    return jnp.repeat(live, width)


def shards(inverse_rows, panels, diag_inverse, pattern, owner_slot):
    n_rows = lax.axis_size("row")
    n_cols = lax.axis_size("col")
    row_index = lax.axis_index("row")
    col_index = lax.axis_index("col")
    rows_here = panels.shape[1]
    cols_here = inverse_rows.shape[0]
    width = panels.shape[2]
    blocks = pattern.shape[1]
    source_col = row_index * n_cols // n_rows
    start_row = row_index * rows_here - source_col * cols_here
    masked_list = []
    colmask_list = []
    for number in range(2):
        mask_rows = block_mask(
            pattern[number], row_index * (blocks // n_rows), blocks // n_rows, width
        )
        mask_cols = block_mask(
            pattern[number], col_index * (blocks // n_cols), blocks // n_cols, width
        )
        held = from_root(panels[0], "col", owner_slot[number])
        masked_list.append(mask_rows[:, None] * held)
        colmask_list.append(mask_cols)
    masked_all = jnp.stack(masked_list)
    colmask_all = jnp.stack(colmask_list)
    partial_value = jnp.einsum(
        "ij,sjw->siw", inverse_rows, masked_all, precision=lax.Precision.HIGHEST
    )
    column_total = lax.psum(partial_value, "row")
    column = -(colmask_all[:, :, None] * column_total)
    piece = lax.dynamic_slice_in_dim(column, start_row, rows_here, 1)
    lower = from_root(piece, "col", source_col)
    inner = jnp.einsum("sjw,sjv->swv", masked_all, lower, precision=lax.Precision.HIGHEST)
    diagonal = diag_inverse - lax.psum(inner, "row")
    return (lower, jnp.swapaxes(column, 1, 2), diagonal)


def solution(mesh):
    in_specs = (P("col", "row"), P("col", "row", None), P(), P(), P())
    out_specs = (P(None, "row", None), P(None, None, "col"), P())
    return jax.shard_map(shards, mesh=mesh, in_specs=in_specs, out_specs=out_specs, check_vma=False)
```

profile of v0, /device:TPU:0, one launch (start us, length us, event | category | flops | bytes accessed | tf_op | source)
XLA Modules:
  0.0 592.8 jit_solution(14428068676685210212)
XLA Ops:
  7.2 1.3 fusion.17
  9.8 1.9 copy.8
  11.8 2.5 select_bitcast_fusion.1
  14.4 0.1 fusion.11
  14.5 0.1 broadcast_bitcast_fusion.3
  14.6 0.1 fusion.13
  14.6 0.1 broadcast_bitcast_fusion.2
  14.7 157.5 %all-reduce.12.cloned.1.call-done = (f32[2048,256]{0,1:T(8,128)}, f32[2048,256]{0,1:T(8,128)}) async-done(((f32[2048,256]{0,1:T(8,128)}, f32[2048,256]{0,1:T(8,128)}), (f32[2048,256]{0,1:T(8,128)}, f32[2048,256]{0,1:T(8,128)})) %all-reduce.12.cloned.1.call-update) | async-done | bytes 4194320 | tf_op jit(solution)/shard_map/psum | solution.py:9
  172.2 2.6 multiply_bitcast_fusion
  174.8 1.3 copy-done
  176.1 59.4 %fusion.2 = f32[2,4096,256]{1,2,0:T(8,128)} fusion(f32[4096,2048]{1,0:T(8,128)} %param.5, f32[1,2048,256]{1,2,0:T(8,128)S(1)} %get-tuple-element.14, f32[1,2048,256]{1,2,0:T(8,128)S(1)} %get-tuple-element.15), kind=kOutput, calls=%fused_computation.3 | convolution fusion | flops 51540656128 | bytes 46137344 | tf_op jit(solution)/shard_map/ij,sjw->siw/dot_general | solution.py:42
  235.5 0.0 all-reduce.8.cloned.1.call-start
  235.6 0.1 fusion.7
  235.7 0.1 broadcast_bitcast_fusion.1
  235.8 0.1 broadcast_bitcast_fusion
  235.9 125.0 %all-reduce.6.cloned.1.call-done = f32[2,4096,256]{1,2,0:T(8,128)} async-done(((f32[2,4096,256]{1,2,0:T(8,128)}), f32[2,4096,256]{1,2,0:T(8,128)}) %all-reduce.6.cloned.1.call-update) | async-done | bytes 8388624 | tf_op jit(solution)/shard_map/psum | solution.py:45
  360.9 4.3 multiply_negate_fusion
  365.2 2.3 dynamic-slice_select_fusion
  367.6 155.2 %all-reduce.8.cloned.1.call-done = f32[2,2048,256]{1,2,0:T(8,128)} async-done(((f32[2,2048,256]{1,2,0:T(8,128)}), f32[2,2048,256]{1,2,0:T(8,128)}) %all-reduce.8.cloned.1.call-update) | async-done | bytes 4194320 | tf_op jit(solution)/shard_map/psum | solution.py:9
  522.8 7.6 %fusion.5 = f32[2,256,256]{2,1,0:T(8,128)} fusion(f32[2,2048,256]{1,2,0:T(8,128)} %all-reduce.8.cloned.1.call-done, f32[1,2048,256]{1,2,0:T(8,128)S(1)} %get-tuple-element.14, f32[1,2048,256]{1,2,0:T(8,128)} %copy-done), kind=kOutput, calls=%fused_computation.6 | convolution fusion | flops 3222274048 | bytes 8912896 | tf_op jit(solution)/shard_map/sjw,sjv->swv/dot_general | solution.py:49
  530.4 8.3 %fusion.19 = f32[2,256,4096]{2,1,0:T(8,128)} fusion(f32[2,4096,256]{1,2,0:T(8,128)} %all-reduce.6.cloned.1.call-done, f32[2,4096]{1,0:T(2,128)S(1)} %pad_maximum_fusion.3), kind=kLoop, calls=%fused_computation.32 | loop fusion | flops 4194304 | bytes 16809984 | tf_op jit(solution)/shard_map/transpose | solution.py:51
  538.7 5.4 copy.11
  544.1 40.2 %all-reduce.10.cloned.1.call-done = f32[2,256,256]{2,1,0:T(8,128)} async-done(((f32[2,256,256]{2,1,0:T(8,128)}), f32[2,256,256]{2,1,0:T(8,128)}) %all-reduce.10.cloned.1.call-update) | async-done | bytes 524304 | tf_op jit(solution)/shard_map/psum | solution.py:50
  584.3 1.9 sub.12
  (18 shorter events, 0.3 us)
Async XLA Ops:
  7.2 165.1 %all-reduce.12.cloned.1.call-start = ((), (), s32[]{:S(2)}) async-start(), calls=%async_computation.3 | async-start | bytes 8388608 | tf_op jit(solution)/shard_map/psum | solution.py:9
  11.8 2.6 copy-start.2
  14.3 346.6 %all-reduce.6.cloned.1.call-start = ((), (), s32[]{:S(2)}) async-start(), calls=%async_computation | async-start | bytes 16777216 | tf_op jit(solution)/shard_map/psum | solution.py:45
  174.8 1.3 copy-start
  235.5 287.3 %all-reduce.8.cloned.1.call-start = ((), (), s32[]{:S(2)}) async-start(), calls=%async_computation.1 | async-start | bytes 8388608 | tf_op jit(solution)/shard_map/psum | solution.py:9
  367.5 216.8 %all-reduce.10.cloned.1.call-start = ((), (), s32[]{:S(2)}) async-start(), calls=%async_computation.2 | async-start | bytes 1048576 | tf_op jit(solution)/shard_map/psum | solution.py:50
  538.7 45.6 %copy-start.1 = (f32[2,256,256]{2,1,0:T(8,128)S(1)}, f32[2,256,256]{2,1,0:T(8,128)}, u32[]{:S(2)}) copy-start(f32[2,256,256]{2,1,0:T(8,128)} %param.7) | copy-start | bytes 1572868
Sparse Core Ops, SparseCore 0:
  14.4 157.7 all-reduce.11
  235.7 125.1 all-reduce.5
  367.7 155.1 all-reduce.7
  530.5 53.7 all-reduce.9
where the time goes:
time: 593 us
  waiting for transfers between devices  478 us (81%)
  matrix products  67 us (11%)
  other arithmetic  22.1 us (4%)
  between operations  15.2 us (3%)
  local copies, waits for them, and re-layouts  10.3 us (2%)
    psum x2, waiting for transfers between devices, from_root(): return lax.psum(jnp.where(mine, array, jnp.zeros_like(array)), axis)  313 us
    psum x1, waiting for transfers between devices, shards(): column_total = lax.psum(partial_value, 'row')  125 us
    dot_general x1, matrix products, shards(): jnp.einsum('ij,sjw->siw', inverse_rows, masked_all, precision=lax.Precisi...  59.4 us
    psum x1, waiting for transfers between devices, shards(): diagonal = diag_inverse - lax.psum(inner, 'row')  40.2 us
  transfers between devices with their start and end apart: 4, of which 4 were waited for; matrix products, arithmetic and copies ran while one was open for 2% of the time, Pallas kernels for 0%

commit v1 on v0

--- a/solution.py
+++ b/solution.py
@@ -15,6 +15,17 @@
 
 
 def shards(inverse_rows, panels, diag_inverse, pattern, owner_slot):
+
+    def create_the_sectors(local_array, row_axis):
+        dev_count = lax.axis_size(row_axis)
+        back, b_now = (local_array, 0)
+        while 1 << b_now < dev_count:
+            shaped = tuple(((ix, ix ^ 1 << b_now) for ix in range(dev_count)))
+            all_rows = lax.ppermute(back, row_axis, shaped)
+            back = back + all_rows
+            b_now = b_now + 1
+        return back
+
     n_rows = lax.axis_size("row")
     n_cols = lax.axis_size("col")
     row_index = lax.axis_index("row")
@@ -42,7 +53,7 @@
     partial_value = jnp.einsum(
         "ij,sjw->siw", inverse_rows, masked_all, precision=lax.Precision.HIGHEST
     )
-    column_total = lax.psum(partial_value, "row")
+    column_total = create_the_sectors(partial_value, "row")
     column = -(colmask_all[:, :, None] * column_total)
     piece = lax.dynamic_slice_in_dim(column, start_row, rows_here, 1)
     lower = from_root(piece, "col", source_col)

time: 593 us -> 879 us (1.48)
  waiting for transfers between devices: 478 us -> 735 us
  other arithmetic: 22.1 us -> 46.4 us
    ppermute x0 -> x3, waiting for transfers between devices: none -> 375 us  [create_the_sectors(): all_rows = lax.ppermute(back, row_axis, shaped)]
    psum x1 -> x0, waiting for transfers between devices: 125 us -> none  [shards(): column_total = lax.psum(partial_value, 'row')]
    add x0 -> x2, other arithmetic: none -> 22.6 us  [create_the_sectors(): back = back + all_rows]
  transfers between devices with their start and end apart: 4 -> 6, of which waited for: 4 -> 6; matrix products, arithmetic and copies ran while one was open for 2% -> 1% of each run, Pallas kernels for 0% -> 0%
where the time goes in v1:
time: 879 us
  waiting for transfers between devices  735 us (84%)
  matrix products  66.6 us (8%)
  other arithmetic  46.4 us (5%)
  between operations  15.2 us (2%)
  local copies, waits for them, and re-layouts  12.4 us (1%)
    ppermute x3, waiting for transfers between devices, create_the_sectors(): all_rows = lax.ppermute(back, row_axis, shaped)  375 us
    psum x2, waiting for transfers between devices, from_root(): return lax.psum(jnp.where(mine, array, jnp.zeros_like(array)), axis)  312 us
    dot_general x1, matrix products, shards(): jnp.einsum('ij,sjw->siw', inverse_rows, masked_all, precision=lax.Precisi...  59.1 us
    psum x1, waiting for transfers between devices, shards(): diagonal = diag_inverse - lax.psum(inner, 'row')  48.5 us
    add x2, other arithmetic, create_the_sectors(): back = back + all_rows  22.6 us
  transfers between devices with their start and end apart: 6, of which 6 were waited for; matrix products, arithmetic and copies ran while one was open for 1% of the time, Pallas kernels for 0%

profile of v1, /device:TPU:0, one launch (start us, length us, event | category | flops | bytes accessed | tf_op | source)
XLA Modules:
  0.0 878.7 jit_solution(15181842736916401670)
XLA Ops:
  7.2 1.3 fusion.17
  9.8 1.9 copy.8
  11.8 2.5 select_bitcast_fusion.1
  14.4 0.1 fusion.13
  14.6 0.1 fusion.11
  14.7 157.5 %all-reduce.9.cloned.1.call-done = (f32[2048,256]{0,1:T(8,128)}, f32[2048,256]{0,1:T(8,128)}) async-done(((f32[2048,256]{0,1:T(8,128)}, f32[2048,256]{0,1:T(8,128)}), (f32[2048,256]{0,1:T(8,128)}, f32[2048,256]{0,1:T(8,128)})) %all-reduce.9.cloned.1.call-update) | async-done | bytes 4194320 | tf_op jit(solution)/shard_map/psum | solution.py:9
  172.2 2.6 multiply_bitcast_fusion
  174.8 59.1 %fusion.2 = f32[2,4096,256]{1,2,0:T(8,128)S(1)} fusion(f32[4096,2048]{1,0:T(8,128)} %param.5, f32[1,2048,256]{1,2,0:T(8,128)S(1)} %get-tuple-element.14, f32[1,2048,256]{1,2,0:T(8,128)S(1)} %get-tuple-element.15), kind=kOutput, calls=%fused_computation.3 | convolution fusion | flops 51540656128 | bytes 46137344 | tf_op jit(solution)/shard_map/ij,sjw->siw/dot_general | solution.py:53
  233.9 3.4 copy-done
  237.3 13.3 %collective-permute-done = f32[2,4096,256]{1,2,0:T(8,128)} collective-permute-done((f32[2,4096,256]{1,2,0:T(8,128)S(1)}, f32[2,4096,256]{1,2,0:T(8,128)}, u32[]{:S(2)}, u32[]{:S(2)}) %collective-permute-start) | collective-permute-done | bytes 8388640 | tf_op jit(solution)/shard_map/ppermute | solution.py:24
  250.6 11.3 %add.31 = f32[2,4096,256]{1,2,0:T(8,128)} add(f32[2,4096,256]{1,2,0:T(8,128)} %copy-done, f32[2,4096,256]{1,2,0:T(8,128)} %collective-permute-done) | non-fusion elementwise | flops 2097152 | bytes 25165824 | tf_op jit(solution)/shard_map/add | solution.py:25
  261.9 1.5 collective-permute-start.1
  263.4 181.3 %collective-permute-done.1 = f32[2,4096,256]{1,2,0:T(8,128)} collective-permute-done((f32[2,4096,256]{1,2,0:T(8,128)}, f32[2,4096,256]{1,2,0:T(8,128)}, u32[]{:S(2)}, u32[]{:S(2)}) %collective-permute-start.1) | collective-permute-done | bytes 8388640 | tf_op jit(solution)/shard_map/ppermute | solution.py:24
  444.7 11.3 %add.32 = f32[2,4096,256]{1,2,0:T(8,128)} add(f32[2,4096,256]{1,2,0:T(8,128)} %add.31, f32[2,4096,256]{1,2,0:T(8,128)} %collective-permute-done.1) | non-fusion elementwise | flops 2097152 | bytes 25165824 | tf_op jit(solution)/shard_map/add | solution.py:25
  456.0 1.5 collective-permute-start.2
  457.5 0.1 fusion.7
  457.8 180.2 %collective-permute-done.2 = f32[2,4096,256]{1,2,0:T(8,128)} collective-permute-done((f32[2,4096,256]{1,2,0:T(8,128)}, f32[2,4096,256]{1,2,0:T(8,128)}, u32[]{:S(2)}, u32[]{:S(2)}) %collective-permute-start.2) | collective-permute-done | bytes 8388640 | tf_op jit(solution)/shard_map/ppermute | solution.py:24
  638.0 11.8 %multiply_negate_fusion = f32[2,4096,256]{1,2,0:T(8,128)} fusion(f32[2,4096,256]{1,2,0:T(8,128)} %add.32, f32[2,4096,256]{1,2,0:T(8,128)} %collective-permute-done.2, f32[2,4096]{1,0:T(2,128)S(1)} %pad_maximum_fusion.3), kind=kLoop, calls=%fused_computation.2 | loop fusion | flops 6291456 | bytes 25198592 | tf_op jit(solution)/shard_map/neg | solution.py:57
  649.8 4.7 dynamic-slice_select_fusion
  654.6 154.1 %all-reduce.5.cloned.1.call-done = f32[2,2048,256]{1,2,0:T(8,128)} async-done(((f32[2,2048,256]{1,2,0:T(8,128)}), f32[2,2048,256]{1,2,0:T(8,128)}) %all-reduce.5.cloned.1.call-update) | async-done | bytes 4194320 | tf_op jit(solution)/shard_map/psum | solution.py:9
  808.7 7.6 fusion.5
  816.3 5.4 copy.11
  821.7 48.5 %all-reduce.7.cloned.1.call-done = f32[2,256,256]{2,1,0:T(8,128)} async-done(((f32[2,256,256]{2,1,0:T(8,128)}), f32[2,256,256]{2,1,0:T(8,128)}) %all-reduce.7.cloned.1.call-update) | async-done | bytes 524304 | tf_op jit(solution)/shard_map/psum | solution.py:61
  870.2 1.9 sub.12
  (24 shorter events, 0.6 us)
Async XLA Ops:
  7.2 165.1 %all-reduce.9.cloned.1.call-start = ((), (), s32[]{:S(2)}) async-start(), calls=%async_computation.2 | async-start | bytes 8388608 | tf_op jit(solution)/shard_map/psum | solution.py:9
  11.8 2.6 copy-start.3
  14.3 794.4 %all-reduce.5.cloned.1.call-start = ((), (), s32[]{:S(2)}) async-start(), calls=%async_computation | async-start | bytes 8388608 | tf_op jit(solution)/shard_map/psum | solution.py:9
  174.8 59.1 %copy-start.1 = (f32[1,2048,256]{1,2,0:T(8,128)}, f32[1,2048,256]{1,2,0:T(8,128)S(1)}, u32[]{:S(2)}) copy-start(f32[1,2048,256]{1,2,0:T(8,128)S(1)} %get-tuple-element.15) | copy-start | bytes 6291460
  233.9 3.4 copy-start
  237.3 13.3 %collective-permute-start = (f32[2,4096,256]{1,2,0:T(8,128)S(1)}, f32[2,4096,256]{1,2,0:T(8,128)}, u32[]{:S(2)}, u32[]{:S(2)}) collective-permute-start(f32[2,4096,256]{1,2,0:T(8,128)S(1)} %fusion.2), channel_id=1, source_target_pairs={{0,4},{4,0},{8,12},{12,8},{16,20},{20,16},{24,28},{28,24},{1,5},{5... | collective-permute-start | bytes 25165832 | tf_op jit(solution)/shard_map/ppermute | solution.py:24
  261.9 182.8 %collective-permute-start.1 = (f32[2,4096,256]{1,2,0:T(8,128)}, f32[2,4096,256]{1,2,0:T(8,128)}, u32[]{:S(2)}, u32[]{:S(2)}) collective-permute-start(f32[2,4096,256]{1,2,0:T(8,128)} %add.31), channel_id=1, source_target_pairs={{0,8},{4,12},{8,0},{12,4},{16,24},{20,28},{24,16},{28,20},{1,9},{5... | collective-permute-start | bytes 25165832 | tf_op jit(solution)/shard_map/ppermute | solution.py:24
  456.0 182.0 %collective-permute-start.2 = (f32[2,4096,256]{1,2,0:T(8,128)}, f32[2,4096,256]{1,2,0:T(8,128)}, u32[]{:S(2)}, u32[]{:S(2)}) collective-permute-start(f32[2,4096,256]{1,2,0:T(8,128)} %add.32), channel_id=1, source_target_pairs={{0,16},{4,20},{8,24},{12,28},{16,0},{20,4},{24,8},{28,12},{1,17},{... | collective-permute-start | bytes 25165832 | tf_op jit(solution)/shard_map/ppermute | solution.py:24
  654.6 215.6 %all-reduce.7.cloned.1.call-start = ((), (), s32[]{:S(2)}) async-start(), calls=%async_computation.1 | async-start | bytes 1048576 | tf_op jit(solution)/shard_map/psum | solution.py:61
  816.3 53.9 %copy-start.2 = (f32[2,256,256]{2,1,0:T(8,128)S(1)}, f32[2,256,256]{2,1,0:T(8,128)}, u32[]{:S(2)}) copy-start(f32[2,256,256]{2,1,0:T(8,128)} %param.7) | copy-start | bytes 1572868
Sparse Core Ops, SparseCore 0:
  14.4 157.7 all-reduce.8
  654.7 153.9 all-reduce.4
  816.4 53.7 all-reduce.6
